TPU v7x, 32 devices: a whole 2x2x4 slice. The times are simulated.
32 devices in a mesh: gx: 4 (over x, core), gy: 8 (over z, y).
Axes of the slice: x: 2, y: 2, z: 4, core: 2. Of those that a mesh axis runs over, the one named last changes fastest.
Arguments:
- fields: float32 [9, 32, 128, 128], P(None, 'gx', 'gy'), may hold values from -6 to 6
- labels: int32 [32, 128, 128], P('gx', 'gy'), may hold values from 0 to 7
- buoyancy: float32 [8], replicated, may hold values from 0.15 to 0.35
- lame_first: float32 [8], replicated, may hold values from 0.15 to 0.45
- shear_modulus: float32 [8], replicated, may hold values from 0.05 to 0.2
- relax_rate: float32 [8], replicated, may hold values from 0.02 to 0.3
Outputs:
- advanced: float32 [9, 32, 128, 128], P(None, 'gx', 'gy')
Inputs may be any that keep to these rules, and one draw needn't show every extreme that they name: labels name tissue classes.
All inputs are finite; a program needn't handle non-finite values.
Results may differ from a plain program's by a relative error of at most 0.00002.
Values sent between devices are 32-bit elements; how exact they have to be, the bound alone decides.
A program may use at most 64 MiB of HBM per device.

v0:
```python
import jax
import jax.numpy as jnp
from jax import lax
from jax.sharding import PartitionSpec as P

STEPS = 4
LABELS = 8


def padded_2(block, sides, width):
    for axis, dim in sides:
        count = lax.axis_size(axis)
        forward = [(i, i + 1) for i in range(count - 1)]
        backward = [(target, source) for source, target in forward]
        low = lax.ppermute(
            lax.slice_in_dim(block, block.shape[dim] - width, None, axis=dim), axis, forward
        )
        high = lax.ppermute(lax.slice_in_dim(block, 0, width, axis=dim), axis, backward)
        block = jnp.concatenate([low, block, high], axis=dim)
    return block


def ahead(field, axis):
    count = field.shape[axis]
    zeros = jnp.zeros_like(lax.slice_in_dim(field, 0, 1, axis=axis))
    following = jnp.concatenate([lax.slice_in_dim(field, 1, count, axis=axis), zeros], axis)
    return following - field


def behind(field, axis):
    count = field.shape[axis]
    zeros = jnp.zeros_like(lax.slice_in_dim(field, 0, 1, axis=axis))
    previous = jnp.concatenate([zeros, lax.slice_in_dim(field, 0, count - 1, axis=axis)], axis)
    return field - previous


def speeds_update(state, moduli, inside):
    speed_x, speed_y, speed_z, stress_xx, stress_yy, stress_zz, stress_xy, stress_xz, stress_yz = (
        state
    )
    buoy = moduli[0]
    speed_x = (
        speed_x + buoy * (ahead(stress_xx, 0) + behind(stress_xy, 1) + behind(stress_xz, 2))
    ) * inside
    speed_y = (
        speed_y + buoy * (behind(stress_xy, 0) + ahead(stress_yy, 1) + behind(stress_yz, 2))
    ) * inside
    speed_z = (
        speed_z + buoy * (behind(stress_xz, 0) + behind(stress_yz, 1) + ahead(stress_zz, 2))
    ) * inside
    return [speed_x, speed_y, speed_z]


def stress_update(speeds, stresses, moduli, inside):
    speed_x, speed_y, speed_z = speeds
    stress_xx, stress_yy, stress_zz, stress_xy, stress_xz, stress_yz = stresses
    lame, shear, relax = (moduli[1], moduli[2], moduli[3])
    strain_xx = behind(speed_x, 0)
    strain_yy = behind(speed_y, 1)
    strain_zz = behind(speed_z, 2)
    spread = strain_xx + strain_yy + strain_zz
    keep = 1.0 - relax
    stress_xx = (keep * stress_xx + lame * spread + 2.0 * shear * strain_xx) * inside
    stress_yy = (keep * stress_yy + lame * spread + 2.0 * shear * strain_yy) * inside
    stress_zz = (keep * stress_zz + lame * spread + 2.0 * shear * strain_zz) * inside
    stress_xy = (keep * stress_xy + shear * (ahead(speed_x, 1) + ahead(speed_y, 0))) * inside
    stress_xz = (keep * stress_xz + shear * (ahead(speed_x, 2) + ahead(speed_z, 0))) * inside
    stress_yz = (keep * stress_yz + shear * (ahead(speed_y, 2) + ahead(speed_z, 1))) * inside
    return [stress_xx, stress_yy, stress_zz, stress_xy, stress_xz, stress_yz]


def advance(state, moduli, inside):
    speeds = speeds_update(state, moduli, inside)
    return speeds + stress_update(speeds, state[3:9], moduli, inside)


def lookup(labels, table):
    result = jnp.zeros(labels.shape, jnp.float32)
    for tissue in range(LABELS):
        result = jnp.where(labels == tissue, table[tissue], result)
    return result


def on_device(fields, labels, buoyancy, lame_first, shear_modulus, relax_rate):
    local_x = labels.shape[0]
    local_y = labels.shape[1]
    total_x = local_x * lax.axis_size("gx")
    total_y = local_y * lax.axis_size("gy")
    start_x = lax.axis_index("gx") * local_x
    start_y = lax.axis_index("gy") * local_y
    padded_labels = padded_2(labels, (("gx", 0), ("gy", 1)), 2)
    padded_moduli = [
        lookup(padded_labels, buoyancy),
        lookup(padded_labels, lame_first),
        lookup(padded_labels, shear_modulus),
        lookup(padded_labels, relax_rate),
    ]
    place_x = start_x - 2 + jnp.arange(local_x + 2 * 2, dtype=jnp.int32)
    place_y = start_y - 2 + jnp.arange(local_y + 2 * 2, dtype=jnp.int32)
    within_x = (place_x >= 0) & (place_x < total_x)
    within_y = (place_y >= 0) & (place_y < total_y)
    inside = (within_x[:, None, None] & within_y[None, :, None]).astype(jnp.float32)
    result = fields
    for repeat in range(STEPS):
        padded = padded_2(result, (("gx", 1), ("gy", 2)), 2)
        state = advance([padded[channel] for channel in range(9)], padded_moduli, inside)
        result = jnp.stack(state)[:, 2 : 2 + local_x, 2 : 2 + local_y]
    return result


def solution(mesh):
    placed = (P(None, "gx", "gy", None), P("gx", "gy", None), P(), P(), P(), P())
    return jax.shard_map(
        on_device, mesh=mesh, in_specs=placed, out_specs=P(None, "gx", "gy", None), check_vma=False
    )
```

profile of v0, /device:TPU:9, one launch (start us, length us, event | category | flops | bytes accessed | tf_op | source)
XLA Modules:
  0.0 122.9 jit_solution(11017209157304604422)
XLA Ops:
  1.1 3.7 %collective-permute-start = (f32[9,2,16,128]{3,2,1,0:T(8,128)S(1)}, f32[9,2,16,128]{3,2,1,0:T(8,128)S(1)}, u32[]{:S(2)}, u32[]{:S(2)}) collective-permute-start(f32[9,2,16,128]{3,2,1,0:T(8,128)S(1)} %get-tuple-element.96), channel_id=1, source_target_pairs={{0,8},{8,16},{16,24},{1,9},{9,17},{17,25},{2,10},{10,18},{18,26},{... | collective-permute-start | bytes 442376 | tf_op jit(solution)/shard_map/ppermute | solution.py:15
  4.8 1.9 %collective-permute-start.1 = (f32[9,2,16,128]{3,2,1,0:T(8,128)S(1)}, f32[9,2,16,128]{3,2,1,0:T(8,128)S(1)}, u32[]{:S(2)}, u32[]{:S(2)}) collective-permute-start(f32[9,2,16,128]{3,2,1,0:T(8,128)S(1)} %get-tuple-element.95), channel_id=1, source_target_pairs={{8,0},{16,8},{24,16},{9,1},{17,9},{25,17},{10,2},{18,10},{26,18},{... | collective-permute-start | bytes 442376 | tf_op jit(solution)/shard_map/ppermute | solution.py:18
  7.4 3.6 %collective-permute-start.4 = (s32[2,16,128]{2,1,0:T(8,128)S(1)}, s32[2,16,128]{2,1,0:T(8,128)S(1)}, u32[]{:S(2)}, u32[]{:S(2)}) collective-permute-start(s32[2,16,128]{2,1,0:T(8,128)S(1)} %get-tuple-element.100), channel_id=1, source_target_pairs={{0,8},{8,16},{16,24},{1,9},{9,17},{17,25},{2,10},{10,18},{18,26},{... | collective-permute-start | bytes 49160 | tf_op jit(solution)/shard_map/ppermute | solution.py:15
  20.7 3.1 %collective-permute-start.2 = (f32[9,12,2,128]{3,2,1,0:T(2,128)S(1)}, f32[9,12,2,128]{3,2,1,0:T(2,128)S(1)}, u32[]{:S(2)}, u32[]{:S(2)}) collective-permute-start(f32[9,12,2,128]{3,2,1,0:T(2,128)S(1)} %get-tuple-element.93), channel_id=1, source_target_pairs={{0,1},{1,2},{2,3},{3,4},{4,5},{5,6},{6,7},{8,9},{9,10},{10,11},{11... | collective-permute-start | bytes 331784 | tf_op jit(solution)/shard_map/ppermute | solution.py:15
  23.8 3.0 %collective-permute-start.3 = (f32[9,12,2,128]{3,2,1,0:T(2,128)S(1)}, f32[9,12,2,128]{3,2,1,0:T(2,128)S(1)}, u32[]{:S(2)}, u32[]{:S(2)}) collective-permute-start(f32[9,12,2,128]{3,2,1,0:T(2,128)S(1)} %get-tuple-element.94), channel_id=1, source_target_pairs={{1,0},{2,1},{3,2},{4,3},{5,4},{6,5},{7,6},{9,8},{10,9},{11,10},{12... | collective-permute-start | bytes 331784 | tf_op jit(solution)/shard_map/ppermute | solution.py:18
  26.9 2.2 %collective-permute-start.6 = (s32[12,2,128]{2,1,0:T(2,128)S(1)}, s32[12,2,128]{2,1,0:T(2,128)S(1)}, u32[]{:S(2)}, u32[]{:S(2)}) collective-permute-start(s32[12,2,128]{2,1,0:T(2,128)S(1)} %get-tuple-element.97), channel_id=1, source_target_pairs={{0,1},{1,2},{2,3},{3,4},{4,5},{5,6},{6,7},{8,9},{9,10},{10,11},{11... | collective-permute-start | bytes 36872 | tf_op jit(solution)/shard_map/ppermute | solution.py:15
  29.1 3.9 %collective-permute-start.7 = (s32[12,2,128]{2,1,0:T(2,128)S(1)}, s32[12,2,128]{2,1,0:T(2,128)S(1)}, u32[]{:S(2)}, u32[]{:S(2)}) collective-permute-start(s32[12,2,128]{2,1,0:T(2,128)S(1)} %get-tuple-element.98), channel_id=1, source_target_pairs={{1,0},{2,1},{3,2},{4,3},{5,4},{6,5},{7,6},{9,8},{10,9},{11,10},{12... | collective-permute-start | bytes 36872 | tf_op jit(solution)/shard_map/ppermute | solution.py:18
  34.3 5.3 %bitcast_dynamic-update-slice_fusion.35 = (f32[9,12,20,128]{3,2,1,0:T(8,128)S(1)}, f32[12,20,128]{2,1,0:T(8,128)S(1)}, f32[12,20,128]{2,1,0:T(8,128)S(1)}, pred[...) fusion(f32[12,20]{1,0:T(8,128)S(1)} %and_convert_fusion, ...), kind=kLoop, calls=%fused_computation.100 | loop fusion | flops 798719 | bytes 1703968
  40.3 15.4 %bitcast_dynamic-update-slice_fusion.32 = (f32[9,12,20,128]{3,2,1,0:T(8,128)S(1)}, f32[12,20,128]{2,1,0:T(8,128)S(1)}, f32[12,20,128]{2,1,0:T(8,128)S(1)}, f32[12,20,128]{2,1,0:T(8,128)S(1)}, f32[12,20,128]{2,1,0:T(8,128)S(1)}) fusion(f32[9,12,20,128]{3,2,1,0:T(8,128)S(1)} %get-tuple-element.34, f32[9,12,20,128]{3,2,1,0:T(8,128)S(1)} %pad_maximum_fusion, ...), kind=kLoop, calls=%fused_computation.97 | loop fusion | flops 1136640 | bytes 2060384
  56.3 5.4 %collective-permute-start.8 = (f32[9,2,16,128]{3,2,1,0:T(8,128)S(1)}, f32[9,2,16,128]{3,2,1,0:T(8,128)S(1)}, u32[]{:S(2)}, u32[]{:S(2)}) collective-permute-start(f32[9,2,16,128]{3,2,1,0:T(8,128)S(1)} %get-tuple-element.77), channel_id=1, source_target_pairs={{0,8},{8,16},{16,24},{1,9},{9,17},{17,25},{2,10},{10,18},{18,26},{... | collective-permute-start | bytes 442376 | tf_op jit(solution)/shard_map/ppermute | solution.py:15
  61.7 1.9 %collective-permute-start.9 = (f32[9,2,16,128]{3,2,1,0:T(8,128)S(1)}, f32[9,2,16,128]{3,2,1,0:T(8,128)S(1)}, u32[]{:S(2)}, u32[]{:S(2)}) collective-permute-start(f32[9,2,16,128]{3,2,1,0:T(8,128)S(1)} %get-tuple-element.78), channel_id=1, source_target_pairs={{8,0},{16,8},{24,16},{9,1},{17,9},{25,17},{10,2},{18,10},{26,18},{... | collective-permute-start | bytes 442376 | tf_op jit(solution)/shard_map/ppermute | solution.py:18
  63.8 4.4 %collective-permute-done.9 = f32[9,2,16,128]{3,2,1,0:T(8,128)S(1)} collective-permute-done((f32[9,2,16,128]{3,2,1,0:T(8,128)S(1)}, f32[9,2,16,128]{3,2,1,0:T(8,128)S(1)}, u32[]{:S(2)}, u32[]{:S(2)}) %collective-permute-start.9) | collective-permute-done | bytes 147488 | tf_op jit(solution)/shard_map/ppermute | solution.py:18
  68.2 4.5 %collective-permute-start.10 = (f32[9,12,2,128]{3,2,1,0:T(2,128)S(1)}, f32[9,12,2,128]{3,2,1,0:T(2,128)S(1)}, u32[]{:S(2)}, u32[]{:S(2)}) collective-permute-start(f32[9,12,2,128]{3,2,1,0:T(2,128)S(1)} %get-tuple-element.91), channel_id=1, source_target_pairs={{0,1},{1,2},{2,3},{3,4},{4,5},{5,6},{6,7},{8,9},{9,10},{10,11},{11... | collective-permute-start | bytes 331784 | tf_op jit(solution)/shard_map/ppermute | solution.py:15
  75.7 2.6 %collective-permute-done.11 = f32[9,12,2,128]{3,2,1,0:T(2,128)S(1)} collective-permute-done((f32[9,12,2,128]{3,2,1,0:T(2,128)S(1)}, f32[9,12,2,128]{3,2,1,0:T(2,128)S(1)}, u32[]{:S(2)}, u32[]{:S(2)}) %collective-permute-start.11) | collective-permute-done | bytes 110624 | tf_op jit(solution)/shard_map/ppermute | solution.py:18
  80.3 3.2 %collective-permute-start.12 = (f32[9,2,16,128]{3,2,1,0:T(8,128)S(1)}, f32[9,2,16,128]{3,2,1,0:T(8,128)S(1)}, u32[]{:S(2)}, u32[]{:S(2)}) collective-permute-start(f32[9,2,16,128]{3,2,1,0:T(8,128)S(1)} %get-tuple-element.67), channel_id=1, source_target_pairs={{0,8},{8,16},{16,24},{1,9},{9,17},{17,25},{2,10},{10,18},{18,26},{... | collective-permute-start | bytes 442376 | tf_op jit(solution)/shard_map/ppermute | solution.py:15
  85.6 4.4 %collective-permute-done.13 = f32[9,2,16,128]{3,2,1,0:T(8,128)S(1)} collective-permute-done((f32[9,2,16,128]{3,2,1,0:T(8,128)S(1)}, f32[9,2,16,128]{3,2,1,0:T(8,128)S(1)}, u32[]{:S(2)}, u32[]{:S(2)}) %collective-permute-start.13) | collective-permute-done | bytes 147488 | tf_op jit(solution)/shard_map/ppermute | solution.py:18
  90.1 2.7 %collective-permute-start.14 = (f32[9,12,2,128]{3,2,1,0:T(2,128)S(1)}, f32[9,12,2,128]{3,2,1,0:T(2,128)S(1)}, u32[]{:S(2)}, u32[]{:S(2)}) collective-permute-start(f32[9,12,2,128]{3,2,1,0:T(2,128)S(1)} %get-tuple-element.89), channel_id=1, source_target_pairs={{0,1},{1,2},{2,3},{3,4},{4,5},{5,6},{6,7},{8,9},{9,10},{10,11},{11... | collective-permute-start | bytes 331784 | tf_op jit(solution)/shard_map/ppermute | solution.py:15
  92.7 3.5 %collective-permute-start.15 = (f32[9,12,2,128]{3,2,1,0:T(2,128)S(1)}, f32[9,12,2,128]{3,2,1,0:T(2,128)S(1)}, u32[]{:S(2)}, u32[]{:S(2)}) collective-permute-start(f32[9,12,2,128]{3,2,1,0:T(2,128)S(1)} %get-tuple-element.90), channel_id=1, source_target_pairs={{1,0},{2,1},{3,2},{4,3},{5,4},{6,5},{7,6},{9,8},{10,9},{11,10},{12... | collective-permute-start | bytes 331784 | tf_op jit(solution)/shard_map/ppermute | solution.py:18
  96.6 1.9 %collective-permute-done.15 = f32[9,12,2,128]{3,2,1,0:T(2,128)S(1)} collective-permute-done((f32[9,12,2,128]{3,2,1,0:T(2,128)S(1)}, f32[9,12,2,128]{3,2,1,0:T(2,128)S(1)}, u32[]{:S(2)}, u32[]{:S(2)}) %collective-permute-start.15) | collective-permute-done | bytes 110624 | tf_op jit(solution)/shard_map/ppermute | solution.py:18
  100.5 2.9 %collective-permute-start.16 = (f32[9,2,16,128]{3,2,1,0:T(8,128)S(1)}, f32[9,2,16,128]{3,2,1,0:T(8,128)S(1)}, u32[]{:S(2)}, u32[]{:S(2)}) collective-permute-start(f32[9,2,16,128]{3,2,1,0:T(8,128)S(1)} %get-tuple-element.57), channel_id=1, source_target_pairs={{0,8},{8,16},{16,24},{1,9},{9,17},{17,25},{2,10},{10,18},{18,26},{... | collective-permute-start | bytes 442376 | tf_op jit(solution)/shard_map/ppermute | solution.py:15
  103.5 1.9 %collective-permute-start.17 = (f32[9,2,16,128]{3,2,1,0:T(8,128)S(1)}, f32[9,2,16,128]{3,2,1,0:T(8,128)S(1)}, u32[]{:S(2)}, u32[]{:S(2)}) collective-permute-start(f32[9,2,16,128]{3,2,1,0:T(8,128)S(1)} %get-tuple-element.58), channel_id=1, source_target_pairs={{8,0},{16,8},{24,16},{9,1},{17,9},{25,17},{10,2},{18,10},{26,18},{... | collective-permute-start | bytes 442376 | tf_op jit(solution)/shard_map/ppermute | solution.py:18
  105.5 4.4 %collective-permute-done.17 = f32[9,2,16,128]{3,2,1,0:T(8,128)S(1)} collective-permute-done((f32[9,2,16,128]{3,2,1,0:T(8,128)S(1)}, f32[9,2,16,128]{3,2,1,0:T(8,128)S(1)}, u32[]{:S(2)}, u32[]{:S(2)}) %collective-permute-start.17) | collective-permute-done | bytes 147488 | tf_op jit(solution)/shard_map/ppermute | solution.py:18
  110.0 4.5 %collective-permute-start.18 = (f32[9,12,2,128]{3,2,1,0:T(2,128)S(1)}, f32[9,12,2,128]{3,2,1,0:T(2,128)S(1)}, u32[]{:S(2)}, u32[]{:S(2)}) collective-permute-start(f32[9,12,2,128]{3,2,1,0:T(2,128)S(1)} %get-tuple-element.87), channel_id=1, source_target_pairs={{0,1},{1,2},{2,3},{3,4},{4,5},{5,6},{6,7},{8,9},{9,10},{10,11},{11... | collective-permute-start | bytes 331784 | tf_op jit(solution)/shard_map/ppermute | solution.py:15
  117.4 2.6 %collective-permute-done.19 = f32[9,12,2,128]{3,2,1,0:T(2,128)S(1)} collective-permute-done((f32[9,12,2,128]{3,2,1,0:T(2,128)S(1)}, f32[9,12,2,128]{3,2,1,0:T(2,128)S(1)}, u32[]{:S(2)}, u32[]{:S(2)}) %collective-permute-start.19) | collective-permute-done | bytes 110624 | tf_op jit(solution)/shard_map/ppermute | solution.py:18
  (129 shorter events, 28.8 us)
Async XLA Ops:
  0.0 20.5 %copy-start = (f32[9,8,16,128]{3,2,1,0:T(8,128)S(1)}, f32[9,8,16,128]{3,2,1,0:T(8,128)}, u32[]{:S(2)}) copy-start(f32[9,8,16,128]{3,2,1,0:T(8,128)} %param.6) | copy-start | bytes 1769476
  1.1 19.4 %collective-permute-start = (f32[9,2,16,128]{3,2,1,0:T(8,128)S(1)}, f32[9,2,16,128]{3,2,1,0:T(8,128)S(1)}, u32[]{:S(2)}, u32[]{:S(2)}) collective-permute-start(f32[9,2,16,128]{3,2,1,0:T(8,128)S(1)} %get-tuple-element.96), channel_id=1, source_target_pairs={{0,8},{8,16},{16,24},{1,9},{9,17},{17,25},{2,10},{10,18},{18,26},{... | collective-permute-start | bytes 442376 | tf_op jit(solution)/shard_map/ppermute | solution.py:15
  4.8 15.8 %collective-permute-start.1 = (f32[9,2,16,128]{3,2,1,0:T(8,128)S(1)}, f32[9,2,16,128]{3,2,1,0:T(8,128)S(1)}, u32[]{:S(2)}, u32[]{:S(2)}) collective-permute-start(f32[9,2,16,128]{3,2,1,0:T(8,128)S(1)} %get-tuple-element.95), channel_id=1, source_target_pairs={{8,0},{16,8},{24,16},{9,1},{17,9},{25,17},{10,2},{18,10},{26,18},{... | collective-permute-start | bytes 442376 | tf_op jit(solution)/shard_map/ppermute | solution.py:18
  7.4 12.2 %collective-permute-start.4 = (s32[2,16,128]{2,1,0:T(8,128)S(1)}, s32[2,16,128]{2,1,0:T(8,128)S(1)}, u32[]{:S(2)}, u32[]{:S(2)}) collective-permute-start(s32[2,16,128]{2,1,0:T(8,128)S(1)} %get-tuple-element.100), channel_id=1, source_target_pairs={{0,8},{8,16},{16,24},{1,9},{9,17},{17,25},{2,10},{10,18},{18,26},{... | collective-permute-start | bytes 49160 | tf_op jit(solution)/shard_map/ppermute | solution.py:15
  11.1 9.4 %collective-permute-start.5 = (s32[2,16,128]{2,1,0:T(8,128)S(1)}, s32[2,16,128]{2,1,0:T(8,128)S(1)}, u32[]{:S(2)}, u32[]{:S(2)}) collective-permute-start(s32[2,16,128]{2,1,0:T(8,128)S(1)} %get-tuple-element.99), channel_id=1, source_target_pairs={{8,0},{16,8},{24,16},{9,1},{17,9},{25,17},{10,2},{18,10},{26,18},{... | collective-permute-start | bytes 49160 | tf_op jit(solution)/shard_map/ppermute | solution.py:18
  20.7 12.4 %collective-permute-start.2 = (f32[9,12,2,128]{3,2,1,0:T(2,128)S(1)}, f32[9,12,2,128]{3,2,1,0:T(2,128)S(1)}, u32[]{:S(2)}, u32[]{:S(2)}) collective-permute-start(f32[9,12,2,128]{3,2,1,0:T(2,128)S(1)} %get-tuple-element.93), channel_id=1, source_target_pairs={{0,1},{1,2},{2,3},{3,4},{4,5},{5,6},{6,7},{8,9},{9,10},{10,11},{11... | collective-permute-start | bytes 331784 | tf_op jit(solution)/shard_map/ppermute | solution.py:15
  23.8 9.3 %collective-permute-start.3 = (f32[9,12,2,128]{3,2,1,0:T(2,128)S(1)}, f32[9,12,2,128]{3,2,1,0:T(2,128)S(1)}, u32[]{:S(2)}, u32[]{:S(2)}) collective-permute-start(f32[9,12,2,128]{3,2,1,0:T(2,128)S(1)} %get-tuple-element.94), channel_id=1, source_target_pairs={{1,0},{2,1},{3,2},{4,3},{5,4},{6,5},{7,6},{9,8},{10,9},{11,10},{12... | collective-permute-start | bytes 331784 | tf_op jit(solution)/shard_map/ppermute | solution.py:18
  26.9 6.5 %collective-permute-start.6 = (s32[12,2,128]{2,1,0:T(2,128)S(1)}, s32[12,2,128]{2,1,0:T(2,128)S(1)}, u32[]{:S(2)}, u32[]{:S(2)}) collective-permute-start(s32[12,2,128]{2,1,0:T(2,128)S(1)} %get-tuple-element.97), channel_id=1, source_target_pairs={{0,1},{1,2},{2,3},{3,4},{4,5},{5,6},{6,7},{8,9},{9,10},{10,11},{11... | collective-permute-start | bytes 36872 | tf_op jit(solution)/shard_map/ppermute | solution.py:15
  29.1 5.1 %collective-permute-start.7 = (s32[12,2,128]{2,1,0:T(2,128)S(1)}, s32[12,2,128]{2,1,0:T(2,128)S(1)}, u32[]{:S(2)}, u32[]{:S(2)}) collective-permute-start(s32[12,2,128]{2,1,0:T(2,128)S(1)} %get-tuple-element.98), channel_id=1, source_target_pairs={{1,0},{2,1},{3,2},{4,3},{5,4},{6,5},{7,6},{9,8},{10,9},{11,10},{12... | collective-permute-start | bytes 36872 | tf_op jit(solution)/shard_map/ppermute | solution.py:18
  56.3 7.4 %collective-permute-start.8 = (f32[9,2,16,128]{3,2,1,0:T(8,128)S(1)}, f32[9,2,16,128]{3,2,1,0:T(8,128)S(1)}, u32[]{:S(2)}, u32[]{:S(2)}) collective-permute-start(f32[9,2,16,128]{3,2,1,0:T(8,128)S(1)} %get-tuple-element.77), channel_id=1, source_target_pairs={{0,8},{8,16},{16,24},{1,9},{9,17},{17,25},{2,10},{10,18},{18,26},{... | collective-permute-start | bytes 442376 | tf_op jit(solution)/shard_map/ppermute | solution.py:15
  61.7 6.5 %collective-permute-start.9 = (f32[9,2,16,128]{3,2,1,0:T(8,128)S(1)}, f32[9,2,16,128]{3,2,1,0:T(8,128)S(1)}, u32[]{:S(2)}, u32[]{:S(2)}) collective-permute-start(f32[9,2,16,128]{3,2,1,0:T(8,128)S(1)} %get-tuple-element.78), channel_id=1, source_target_pairs={{8,0},{16,8},{24,16},{9,1},{17,9},{25,17},{10,2},{18,10},{26,18},{... | collective-permute-start | bytes 442376 | tf_op jit(solution)/shard_map/ppermute | solution.py:18
  68.2 7.4 %collective-permute-start.10 = (f32[9,12,2,128]{3,2,1,0:T(2,128)S(1)}, f32[9,12,2,128]{3,2,1,0:T(2,128)S(1)}, u32[]{:S(2)}, u32[]{:S(2)}) collective-permute-start(f32[9,12,2,128]{3,2,1,0:T(2,128)S(1)} %get-tuple-element.91), channel_id=1, source_target_pairs={{0,1},{1,2},{2,3},{3,4},{4,5},{5,6},{6,7},{8,9},{9,10},{10,11},{11... | collective-permute-start | bytes 331784 | tf_op jit(solution)/shard_map/ppermute | solution.py:15
  72.8 5.5 %collective-permute-start.11 = (f32[9,12,2,128]{3,2,1,0:T(2,128)S(1)}, f32[9,12,2,128]{3,2,1,0:T(2,128)S(1)}, u32[]{:S(2)}, u32[]{:S(2)}) collective-permute-start(f32[9,12,2,128]{3,2,1,0:T(2,128)S(1)} %get-tuple-element.92), channel_id=1, source_target_pairs={{1,0},{2,1},{3,2},{4,3},{5,4},{6,5},{7,6},{9,8},{10,9},{11,10},{12... | collective-permute-start | bytes 331784 | tf_op jit(solution)/shard_map/ppermute | solution.py:18
  80.3 5.3 %collective-permute-start.12 = (f32[9,2,16,128]{3,2,1,0:T(8,128)S(1)}, f32[9,2,16,128]{3,2,1,0:T(8,128)S(1)}, u32[]{:S(2)}, u32[]{:S(2)}) collective-permute-start(f32[9,2,16,128]{3,2,1,0:T(8,128)S(1)} %get-tuple-element.67), channel_id=1, source_target_pairs={{0,8},{8,16},{16,24},{1,9},{9,17},{17,25},{2,10},{10,18},{18,26},{... | collective-permute-start | bytes 442376 | tf_op jit(solution)/shard_map/ppermute | solution.py:15
  83.5 6.5 %collective-permute-start.13 = (f32[9,2,16,128]{3,2,1,0:T(8,128)S(1)}, f32[9,2,16,128]{3,2,1,0:T(8,128)S(1)}, u32[]{:S(2)}, u32[]{:S(2)}) collective-permute-start(f32[9,2,16,128]{3,2,1,0:T(8,128)S(1)} %get-tuple-element.68), channel_id=1, source_target_pairs={{8,0},{16,8},{24,16},{9,1},{17,9},{25,17},{10,2},{18,10},{26,18},{... | collective-permute-start | bytes 442376 | tf_op jit(solution)/shard_map/ppermute | solution.py:18
  90.1 6.5 %collective-permute-start.14 = (f32[9,12,2,128]{3,2,1,0:T(2,128)S(1)}, f32[9,12,2,128]{3,2,1,0:T(2,128)S(1)}, u32[]{:S(2)}, u32[]{:S(2)}) collective-permute-start(f32[9,12,2,128]{3,2,1,0:T(2,128)S(1)} %get-tuple-element.89), channel_id=1, source_target_pairs={{0,1},{1,2},{2,3},{3,4},{4,5},{5,6},{6,7},{8,9},{9,10},{10,11},{11... | collective-permute-start | bytes 331784 | tf_op jit(solution)/shard_map/ppermute | solution.py:15
  92.7 5.8 %collective-permute-start.15 = (f32[9,12,2,128]{3,2,1,0:T(2,128)S(1)}, f32[9,12,2,128]{3,2,1,0:T(2,128)S(1)}, u32[]{:S(2)}, u32[]{:S(2)}) collective-permute-start(f32[9,12,2,128]{3,2,1,0:T(2,128)S(1)} %get-tuple-element.90), channel_id=1, source_target_pairs={{1,0},{2,1},{3,2},{4,3},{5,4},{6,5},{7,6},{9,8},{10,9},{11,10},{12... | collective-permute-start | bytes 331784 | tf_op jit(solution)/shard_map/ppermute | solution.py:18
  100.5 5.0 %collective-permute-start.16 = (f32[9,2,16,128]{3,2,1,0:T(8,128)S(1)}, f32[9,2,16,128]{3,2,1,0:T(8,128)S(1)}, u32[]{:S(2)}, u32[]{:S(2)}) collective-permute-start(f32[9,2,16,128]{3,2,1,0:T(8,128)S(1)} %get-tuple-element.57), channel_id=1, source_target_pairs={{0,8},{8,16},{16,24},{1,9},{9,17},{17,25},{2,10},{10,18},{18,26},{... | collective-permute-start | bytes 442376 | tf_op jit(solution)/shard_map/ppermute | solution.py:15
  103.5 6.5 %collective-permute-start.17 = (f32[9,2,16,128]{3,2,1,0:T(8,128)S(1)}, f32[9,2,16,128]{3,2,1,0:T(8,128)S(1)}, u32[]{:S(2)}, u32[]{:S(2)}) collective-permute-start(f32[9,2,16,128]{3,2,1,0:T(8,128)S(1)} %get-tuple-element.58), channel_id=1, source_target_pairs={{8,0},{16,8},{24,16},{9,1},{17,9},{25,17},{10,2},{18,10},{26,18},{... | collective-permute-start | bytes 442376 | tf_op jit(solution)/shard_map/ppermute | solution.py:18
  110.0 7.4 %collective-permute-start.18 = (f32[9,12,2,128]{3,2,1,0:T(2,128)S(1)}, f32[9,12,2,128]{3,2,1,0:T(2,128)S(1)}, u32[]{:S(2)}, u32[]{:S(2)}) collective-permute-start(f32[9,12,2,128]{3,2,1,0:T(2,128)S(1)} %get-tuple-element.87), channel_id=1, source_target_pairs={{0,1},{1,2},{2,3},{3,4},{4,5},{5,6},{6,7},{8,9},{9,10},{10,11},{11... | collective-permute-start | bytes 331784 | tf_op jit(solution)/shard_map/ppermute | solution.py:15
  114.6 5.5 %collective-permute-start.19 = (f32[9,12,2,128]{3,2,1,0:T(2,128)S(1)}, f32[9,12,2,128]{3,2,1,0:T(2,128)S(1)}, u32[]{:S(2)}, u32[]{:S(2)}) collective-permute-start(f32[9,12,2,128]{3,2,1,0:T(2,128)S(1)} %get-tuple-element.88), channel_id=1, source_target_pairs={{1,0},{2,1},{3,2},{4,3},{5,4},{6,5},{7,6},{9,8},{10,9},{11,10},{12... | collective-permute-start | bytes 331784 | tf_op jit(solution)/shard_map/ppermute | solution.py:18
where the time goes:
time: 125 us; the launch traced here: 123 us
  starting transfers between devices  59.8 us (48%)
  other arithmetic  26.3 us (21%)
  waiting for transfers between devices  23.6 us (19%)
  local copies, waits for them, and re-layouts  12.2 us (10%)
    ppermute x10, starting transfers between devices, padded_2(): lax.ppermute(lax.slice_in_dim(block, block.shape[dim] - width, None, axis...  35.9 us
    unnamed x32, other arithmetic  24.7 us
    ppermute x10, starting transfers between devices, padded_2(): lax.ppermute(lax.slice_in_dim(block, 0, width, axis=dim), axis, backward)  23.9 us
    ppermute x10, waiting for transfers between devices, padded_2(): lax.ppermute(lax.slice_in_dim(block, 0, width, axis=dim), axis, backward)  21.2 us
    slice x4, local copies, waits for them, and re-layouts, lookup(): result = jnp.where(labels == tissue, table[tissue], result)  6.49 us
  transfers between devices with their start and end apart: 20, of which 13 were waited for; matrix products, arithmetic and copies ran while one was open for 7% of the time, Pallas kernels for 0%

commit v1 on v0

v1 whole, which is shorter than its diff:
```python
import functools

import jax
import jax.numpy as jnp
from jax import lax
from jax.experimental import pallas as pl
from jax.experimental.pallas import tpu as pltpu
from jax.sharding import PartitionSpec as P

STEPS = 4
LABELS = 8
HALO = STEPS
BASE = 8
MESH = pl.DeviceIdType.MESH
GROUPS = ((0, 3), (3, 6), (6, 9))
VX, VY, VZ, SXX, SYY, SZZ, SXY, SXZ, SYZ = range(9)


def kernel(nx, ny, fields, labels, buoy_t, lame_t, shear_t, relax_t, out, state, tissue,
           buoy, lame, shear, keep, send_sem, recv_sem, local_sem):
    local_x, local_y = labels.shape[0], labels.shape[1]
    gx, gy = lax.axis_index("gx"), lax.axis_index("gy")
    has = {("gx", -1): gx > 0, ("gx", 1): gx < nx - 1, ("gy", -1): gy > 0, ("gy", 1): gy < ny - 1}
    place = {"gx": gx, "gy": gy}
    x0, x1, x2, x3 = 0, HALO, HALO + local_x, local_x + 2 * HALO
    y0, y1, y2, y3 = BASE, BASE + HALO, BASE + HALO + local_y, BASE + local_y + 2 * HALO

    own = [
        pltpu.make_async_copy(labels, tissue.at[x1:x2, y1:y2], local_sem.at[0]),
        pltpu.make_async_copy(fields, state.at[:, x1:x2, y1:y2], local_sem.at[1]),
    ]
    for copy in own:
        copy.start()

    barrier = pltpu.get_barrier_semaphore()
    for (axis, way), there in has.items():
        @pl.when(there)
        def _(axis=axis, way=way):
            pl.semaphore_signal(barrier, inc=1, device_id={axis: place[axis] + way}, device_id_type=MESH)
    pl.semaphore_wait(barrier, sum(there.astype(jnp.int32) for there in has.values()))

    count = [0]

    def remote(src, dst, axis, way):
        index = count[0]
        count[0] += 1
        return pltpu.make_async_remote_copy(
            src_ref=src, dst_ref=dst, send_sem=send_sem.at[index], recv_sem=recv_sem.at[index],
            device_id={axis: place[axis] + way}, device_id_type=MESH,
        )

    def views(source, padded):
        return {
            ("gy", 1): (source(0, local_x, local_y - HALO, local_y), padded(x1, x2, y0, y1)),
            ("gy", -1): (source(0, local_x, 0, HALO), padded(x1, x2, y2, y3)),
            ("gx", 1): (source(local_x - HALO, local_x, 0, local_y), padded(x0, x1, y1, y2)),
            ("gx", -1): (source(0, HALO, 0, local_y), padded(x2, x3, y1, y2)),
        }

    def corners(padded):
        result = {}
        for side, (low, high) in ((-1, (y0, y1)), (1, (y2, y3))):
            result[side, 1] = (padded(x2 - HALO, x2, low, high), padded(x0, x1, low, high))
            result[side, -1] = (padded(x1, x1 + HALO, low, high), padded(x2, x3, low, high))
        return result

    parts = [(lambda a, b, c, d: labels.at[a:b, c:d], lambda a, b, c, d: tissue.at[a:b, c:d])]
    for first, last in GROUPS:
        parts.append((
            lambda a, b, c, d, first=first, last=last: fields.at[first:last, a:b, c:d],
            lambda a, b, c, d, first=first, last=last: state.at[first:last, a:b, c:d],
        ))
    direct, onward = [], []
    for source, padded in parts:
        direct.append({key: remote(*pair, *key) for key, pair in views(source, padded).items()})
        onward.append({key: remote(*pair, "gx", key[1]) for key, pair in corners(padded).items()})

    for sends in direct:
        for key, copy in sends.items():
            pl.when(has[key])(copy.start)

    def blank(a, b, c, d):
        state[:, a:b, c:d] = jnp.zeros((9, b - a, d - c, state.shape[3]), jnp.float32)
        tissue[a:b, c:d] = jnp.full((b - a, d - c, tissue.shape[2]), LABELS, jnp.int32)

    pl.when(jnp.logical_not(has["gx", -1]))(lambda: blank(x0, x1, y0, y3))
    pl.when(jnp.logical_not(has["gx", 1]))(lambda: blank(x2, x3, y0, y3))
    pl.when(jnp.logical_not(has["gy", -1]))(lambda: blank(x0, x3, y0, y1))
    pl.when(jnp.logical_not(has["gy", 1]))(lambda: blank(x0, x3, y2, y3))

    for sends, passes in zip(direct, onward):
        for side in (-1, 1):
            @pl.when(has["gy", side])
            def _(sends=sends, passes=passes, side=side):
                sends["gy", -side].wait_recv()
                for way in (1, -1):
                    pl.when(has["gx", way])(passes[side, way].start)

    def arrived(index):
        for way in (1, -1):
            pl.when(has["gx", -way])(direct[index]["gx", way].wait_recv)
            for side in (-1, 1):
                pl.when(has["gx", -way] & has["gy", side])(onward[index][side, way].wait_recv)

    own[0].wait()
    arrived(0)
    rows = slice(y0, y3)

    @pl.loop(x0, x3)
    def _(p):
        label = tissue[p, rows]
        tables = [jnp.zeros(label.shape, jnp.float32) for _ in range(4)]
        for kind in range(LABELS):
            here = label == kind
            values = (buoy_t[kind], lame_t[kind], shear_t[kind], 1.0 - relax_t[kind])
            tables = [jnp.where(here, value, old) for value, old in zip(values, tables)]
        buoy[p], lame[p], shear[p], keep[p] = tables

    own[1].wait()
    for index in range(1, len(parts)):
        arrived(index)
    for passes in onward:
        for (side, way), copy in passes.items():
            pl.when(has["gy", side] & has["gx", way])(copy.wait_send)

    lanes = state.shape[3]
    lane = lax.broadcasted_iota(jnp.int32, (y3 - y0, lanes), 1)
    first_z, last_z = lane == 0, lane == lanes - 1

    def load(f, p, low, high, shift=0):
        return state[f, p, low + shift:high + shift]

    def ahead_z(a):
        following = pltpu.roll(a, lanes - 1, 1)
        return jnp.where(last_z[:a.shape[0]], 0.0, following) - a

    def behind_z(a):
        return a - jnp.where(first_z[:a.shape[0]], 0.0, pltpu.roll(a, 1, 1))

    for left in range(STEPS, 0, -1):
        low, high = x1 - left, x2 + left - 2

        @pl.loop(low, high + 1)
        def _(p):
            get = lambda f, q, shift=0: load(f, q, y0, y3, shift)
            q = p + 1
            sxy, sxz = get(SXY, p), get(SXZ, p)
            state[VX, p, rows] = get(VX, p) + buoy[p] * (
                get(SXX, q) - get(SXX, p) + (sxy - get(SXY, p, -1)) + behind_z(sxz))
            syz = get(SYZ, q)
            state[VY, q, rows] = get(VY, q) + buoy[q] * (
                get(SXY, q) - sxy + (get(SYY, q, 1) - get(SYY, q)) + behind_z(syz))
            state[VZ, q, rows] = get(VZ, q) + buoy[q] * (
                get(SXZ, q) - sxz + (syz - get(SYZ, q, -1)) + ahead_z(get(SZZ, q)))

        last = left == 1

        @pl.loop(low + 1, high + 1)
        def _(p):
            a, b = (y1, y2) if last else (y0, y3)
            get = lambda f, q, shift=0: load(f, q, a, b, shift)
            part = slice(a - y0, b - y0)
            vx, vy, vz = get(VX, p), get(VY, p), get(VZ, p)
            lam, mu, kept = lame[p, part], shear[p, part], keep[p, part]
            exx, eyy, ezz = vx - get(VX, p - 1), vy - get(VY, p, -1), behind_z(vz)
            spread = lam * (exx + eyy + ezz)
            twice = 2.0 * mu
            new = {
                SXX: kept * get(SXX, p) + spread + twice * exx,
                SYY: kept * get(SYY, p) + spread + twice * eyy,
                SZZ: kept * get(SZZ, p) + spread + twice * ezz,
                SXY: kept * get(SXY, p) + mu * (get(VX, p, 1) - vx + (get(VY, p + 1) - vy)),
                SXZ: kept * get(SXZ, p) + mu * (ahead_z(vx) + (get(VZ, p + 1) - vz)),
                SYZ: kept * get(SYZ, p) + mu * (ahead_z(vy) + (get(VZ, p, 1) - vz)),
            }
            if last:
                new.update({VX: vx, VY: vy, VZ: vz})
            for f, value in new.items():
                if last:
                    out[f, p - x1] = value
                else:
                    state[f, p, rows] = value

    for sends in direct:
        for key, copy in sends.items():
            pl.when(has[key])(copy.wait_send)


def on_device(nx, ny, fields, labels, buoyancy, lame_first, shear_modulus, relax_rate):
    local_x, local_y, lanes = labels.shape
    wide = local_x + 2 * HALO
    tall = local_y + 2 * HALO
    padded = 2 * BASE + tall
    copies = 8 * (len(GROUPS) + 1)
    anywhere = pl.BlockSpec(memory_space=pl.ANY)
    table = pl.BlockSpec(memory_space=pltpu.SMEM)
    return pl.pallas_call(
        functools.partial(kernel, nx, ny),
        out_shape=jax.ShapeDtypeStruct(fields.shape, jnp.float32),
        in_specs=[anywhere, anywhere, table, table, table, table],
        out_specs=pl.BlockSpec(memory_space=pltpu.VMEM),
        scratch_shapes=[
            pltpu.VMEM((9, wide, padded, lanes), jnp.float32),
            pltpu.VMEM((wide, padded, lanes), jnp.int32),
            pltpu.VMEM((wide, tall, lanes), jnp.float32),
            pltpu.VMEM((wide, tall, lanes), jnp.float32),
            pltpu.VMEM((wide, tall, lanes), jnp.float32),
            pltpu.VMEM((wide, tall, lanes), jnp.float32),
            pltpu.SemaphoreType.DMA((copies,)),
            pltpu.SemaphoreType.DMA((copies,)),
            pltpu.SemaphoreType.DMA((2,)),
        ],
        compiler_params=pltpu.CompilerParams(collective_id=0, has_side_effects=True),
        name="waves",
    )(fields, labels, buoyancy, lame_first, shear_modulus, relax_rate)


def solution(mesh):
    placed = (P(None, "gx", "gy", None), P("gx", "gy", None), P(), P(), P(), P())
    return jax.shard_map(
        functools.partial(on_device, mesh.shape["gx"], mesh.shape["gy"]),
        mesh=mesh, in_specs=placed, out_specs=P(None, "gx", "gy", None), check_vma=False,
    )
```

time: 125 us -> 25.7 us (0.21); the launches traced: 123 us -> 25.5 us
  starting transfers between devices: 59.8 us -> 0 us
  other arithmetic: 26.3 us -> 0 us
  Pallas kernels: 0 us -> 23.6 us
  waiting for transfers between devices: 23.6 us -> 0 us
  local copies, waits for them, and re-layouts: 12.2 us -> 1.92 us
    ppermute x20 -> x0, starting transfers between devices: 59.8 us -> none  [the longest x10 35.9 us: padded_2(): lax.ppermute(lax.slice_in_dim(block, block.shape[dim] - width, None, axis...]
    unnamed x32 -> x0, other arithmetic: 24.7 us -> none
    ppermute x20 -> x0, waiting for transfers between devices: 23.6 us -> none  [the longest x10 21.2 us: padded_2(): lax.ppermute(lax.slice_in_dim(block, 0, width, axis=dim), axis, backward)]
    pallas_call x0 -> x1, Pallas kernels: none -> 23.6 us  [on_device(): pl.pallas_call(functools.partial(kernel, nx, ny), out_shape=jax.ShapeDtyp...]
    slice x55 -> x0, local copies, waits for them, and re-layouts: 11.1 us -> none  [the longest x4 6.49 us: lookup(): result = jnp.where(labels == tissue, table[tissue], result)]
  transfers between devices with their start and end apart: 20 -> 0, of which waited for: 13 -> 0; matrix products, arithmetic and copies ran while one was open for 7% -> 0% of each run, Pallas kernels for 0% -> 0%
where the time goes in v1:
time: 25.7 us; the launch traced here: 25.5 us
  Pallas kernels  23.6 us (92%)
  local copies, waits for them, and re-layouts  1.92 us (7%)
    pallas_call x1, Pallas kernels, on_device(): pl.pallas_call(functools.partial(kernel, nx, ny), out_shape=jax.ShapeDtyp...  23.6 us
    unnamed x1, local copies, waits for them, and re-layouts  1.92 us

profile of v1, /device:TPU:9, one launch (start us, length us, event | category | flops | bytes accessed | tf_op | source)
XLA Modules:
  0.0 25.5 jit_solution(15984983634882892509)
XLA Ops:
  0.0 23.6 %waves.1 = f32[9,8,16,128]{3,2,1,0:T(8,128)} custom-call(f32[9,8,16,128]{3,2,1,0:T(8,128)} %fields.1, s32[8,16,128]{2,1,0:T(8,128)} %labels.1, f32[8]{0:T(128)} %buoy_t.1, f32[8]{0:T(128)} %lame_t.1, f32[8]{0:T(128)} %shear_t.1, f32[8]{0:T(128)} %relax_t.1), custom_call_target="tpu_custom_call" | custom-call | tf_op jit(solution)/shard_map/waves/pallas_call | solution.py:197
  23.6 1.9 %copy.8 = f32[9,8,16,128]{3,2,1,0:T(8,128)} copy(f32[9,8,16,128]{3,2,1,0:T(8,128)} %waves.1) | data formatting | bytes 1179648

commit v2 on v1

--- a/solution.py
+++ b/solution.py
@@ -88,13 +88,13 @@
     pl.when(jnp.logical_not(has["gy", -1]))(lambda: blank(x0, x3, y0, y1))
     pl.when(jnp.logical_not(has["gy", 1]))(lambda: blank(x0, x3, y2, y3))
 
-    for sends, passes in zip(direct, onward):
+    def pass_on(index):
         for side in (-1, 1):
             @pl.when(has["gy", side])
-            def _(sends=sends, passes=passes, side=side):
-                sends["gy", -side].wait_recv()
+            def _(side=side):
+                direct[index]["gy", -side].wait_recv()
                 for way in (1, -1):
-                    pl.when(has["gx", way])(passes[side, way].start)
+                    pl.when(has["gx", way])(onward[index][side, way].start)
 
     def arrived(index):
         for way in (1, -1):
@@ -102,20 +102,34 @@
             for side in (-1, 1):
                 pl.when(has["gx", -way] & has["gy", side])(onward[index][side, way].wait_recv)
 
+    pass_on(0)
     own[0].wait()
     arrived(0)
     rows = slice(y0, y3)
-
-    @pl.loop(x0, x3)
-    def _(p):
+    pack = 2 if local_x % 2 == 0 else 1
+
+    def each(low, count, body):
+        @pl.loop(0, count // pack)
+        def _(turn):
+            stores = []
+            for extra in range(pack):
+                stores += body(low + turn * pack + extra)
+            for ref, index, value in stores:
+                ref[index] = value
+
+    def look_up(p):
         label = tissue[p, rows]
         tables = [jnp.zeros(label.shape, jnp.float32) for _ in range(4)]
         for kind in range(LABELS):
             here = label == kind
             values = (buoy_t[kind], lame_t[kind], shear_t[kind], 1.0 - relax_t[kind])
             tables = [jnp.where(here, value, old) for value, old in zip(values, tables)]
-        buoy[p], lame[p], shear[p], keep[p] = tables
-
+        return [(ref, (p,), table) for ref, table in zip((buoy, lame, shear, keep), tables)]
+
+    each(x0, x3 - x0, look_up)
+
+    for index in range(1, len(parts)):
+        pass_on(index)
     own[1].wait()
     for index in range(1, len(parts)):
         arrived(index)
@@ -138,25 +152,27 @@
         return a - jnp.where(first_z[:a.shape[0]], 0.0, pltpu.roll(a, 1, 1))
 
     for left in range(STEPS, 0, -1):
-        low, high = x1 - left, x2 + left - 2
-
-        @pl.loop(low, high + 1)
-        def _(p):
+        low = x1 - left
+        span = local_x + 2 * left
+
+        def speeds(p):
             get = lambda f, q, shift=0: load(f, q, y0, y3, shift)
             q = p + 1
             sxy, sxz = get(SXY, p), get(SXZ, p)
-            state[VX, p, rows] = get(VX, p) + buoy[p] * (
+            vx = get(VX, p) + buoy[p] * (
                 get(SXX, q) - get(SXX, p) + (sxy - get(SXY, p, -1)) + behind_z(sxz))
             syz = get(SYZ, q)
-            state[VY, q, rows] = get(VY, q) + buoy[q] * (
+            vy = get(VY, q) + buoy[q] * (
                 get(SXY, q) - sxy + (get(SYY, q, 1) - get(SYY, q)) + behind_z(syz))
-            state[VZ, q, rows] = get(VZ, q) + buoy[q] * (
+            vz = get(VZ, q) + buoy[q] * (
                 get(SXZ, q) - sxz + (syz - get(SYZ, q, -1)) + ahead_z(get(SZZ, q)))
+            return [(state, (VX, p, rows), vx), (state, (VY, q, rows), vy), (state, (VZ, q, rows), vz)]
+
+        each(low, span, speeds)
 
         last = left == 1
 
-        @pl.loop(low + 1, high + 1)
-        def _(p):
+        def stresses(p, last=last):
             a, b = (y1, y2) if last else (y0, y3)
             get = lambda f, q, shift=0: load(f, q, a, b, shift)
             part = slice(a - y0, b - y0)
@@ -175,11 +191,11 @@
             }
             if last:
                 new.update({VX: vx, VY: vy, VZ: vz})
-            for f, value in new.items():
-                if last:
-                    out[f, p - x1] = value
-                else:
-                    state[f, p, rows] = value
+            if last:
+                return [(out, (f, p - x1), value) for f, value in new.items()]
+            return [(state, (f, p, rows), value) for f, value in new.items()]
+
+        each(low + 1, span - 2, stresses)
 
     for sends in direct:
         for key, copy in sends.items():
@@ -196,16 +212,16 @@
     table = pl.BlockSpec(memory_space=pltpu.SMEM)
     return pl.pallas_call(
         functools.partial(kernel, nx, ny),
-        out_shape=jax.ShapeDtypeStruct(fields.shape, jnp.float32),
+        out_shape=pltpu.VMEM(fields.shape, jnp.float32),
         in_specs=[anywhere, anywhere, table, table, table, table],
         out_specs=pl.BlockSpec(memory_space=pltpu.VMEM),
         scratch_shapes=[
-            pltpu.VMEM((9, wide, padded, lanes), jnp.float32),
+            pltpu.VMEM((9, wide + 1, padded, lanes), jnp.float32),
             pltpu.VMEM((wide, padded, lanes), jnp.int32),
-            pltpu.VMEM((wide, tall, lanes), jnp.float32),
-            pltpu.VMEM((wide, tall, lanes), jnp.float32),
-            pltpu.VMEM((wide, tall, lanes), jnp.float32),
-            pltpu.VMEM((wide, tall, lanes), jnp.float32),
+            pltpu.VMEM((wide + 1, tall, lanes), jnp.float32),
+            pltpu.VMEM((wide + 1, tall, lanes), jnp.float32),
+            pltpu.VMEM((wide + 1, tall, lanes), jnp.float32),
+            pltpu.VMEM((wide + 1, tall, lanes), jnp.float32),
             pltpu.SemaphoreType.DMA((copies,)),
             pltpu.SemaphoreType.DMA((copies,)),
             pltpu.SemaphoreType.DMA((2,)),

time: 25.7 us -> 21.4 us (0.83)
  Pallas kernels: 23.6 us -> 20.2 us
  local copies, waits for them, and re-layouts: 1.92 us -> 0.82 us
    pallas_call x1, Pallas kernels: 23.6 us -> 20.2 us  [on_device(): pl.pallas_call(functools.partial(kernel, nx, ny), out_shape=pltpu.VMEM(fi...]
    unnamed x1, local copies, waits for them, and re-layouts: 1.92 us -> 0.82 us
where the time goes in v2:
time: 21.4 us; the launch traced here: 21.1 us
  Pallas kernels  20.2 us (94%)
  local copies, waits for them, and re-layouts  0.82 us (4%)
    pallas_call x1, Pallas kernels, on_device(): pl.pallas_call(functools.partial(kernel, nx, ny), out_shape=pltpu.VMEM(fi...  20.2 us
    unnamed x1, local copies, waits for them, and re-layouts  0.82 us

profile of v2, /device:TPU:9, one launch (start us, length us, event | category | flops | bytes accessed | tf_op | source)
XLA Modules:
  0.0 21.1 jit_solution(16302862713021405992)
XLA Ops:
  0.0 20.2 %waves.1 = f32[9,8,16,128]{3,2,1,0:T(8,128)S(1)} custom-call(f32[9,8,16,128]{3,2,1,0:T(8,128)} %fields.1, s32[8,16,128]{2,1,0:T(8,128)} %labels.1, f32[8]{0:T(128)} %buoy_t.1, f32[8]{0:T(128)} %lame_t.1, f32[8]{0:T(128)} %shear_t.1, f32[8]{0:T(128)} %relax_t.1), custom_call_target="tpu_custom_call" | custom-call | tf_op jit(solution)/shard_map/waves/pallas_call | solution.py:213
  20.3 0.8 %copy.8 = f32[9,8,16,128]{3,2,1,0:T(8,128)} copy(f32[9,8,16,128]{3,2,1,0:T(8,128)S(1)} %waves.1) | data formatting | bytes 1179648

commit v3 on v2

--- a/solution.py
+++ b/solution.py
@@ -131,10 +131,9 @@
     for index in range(1, len(parts)):
         pass_on(index)
     own[1].wait()
-    for index in range(1, len(parts)):
-        arrived(index)
-    for passes in onward:
-        for (side, way), copy in passes.items():
+
+    def sent(index):
+        for (side, way), copy in onward[index].items():
             pl.when(has["gy", side] & has["gx", way])(copy.wait_send)
 
     lanes = state.shape[3]
@@ -151,51 +150,69 @@
     def behind_z(a):
         return a - jnp.where(first_z[:a.shape[0]], 0.0, pltpu.roll(a, 1, 1))
 
-    for left in range(STEPS, 0, -1):
-        low = x1 - left
-        span = local_x + 2 * left
-
-        def speeds(p):
-            get = lambda f, q, shift=0: load(f, q, y0, y3, shift)
-            q = p + 1
-            sxy, sxz = get(SXY, p), get(SXZ, p)
-            vx = get(VX, p) + buoy[p] * (
-                get(SXX, q) - get(SXX, p) + (sxy - get(SXY, p, -1)) + behind_z(sxz))
-            syz = get(SYZ, q)
-            vy = get(VY, q) + buoy[q] * (
-                get(SXY, q) - sxy + (get(SYY, q, 1) - get(SYY, q)) + behind_z(syz))
-            vz = get(VZ, q) + buoy[q] * (
-                get(SXZ, q) - sxz + (syz - get(SYZ, q, -1)) + ahead_z(get(SZZ, q)))
-            return [(state, (VX, p, rows), vx), (state, (VY, q, rows), vy), (state, (VZ, q, rows), vz)]
-
-        each(low, span, speeds)
-
-        last = left == 1
-
-        def stresses(p, last=last):
-            a, b = (y1, y2) if last else (y0, y3)
-            get = lambda f, q, shift=0: load(f, q, a, b, shift)
-            part = slice(a - y0, b - y0)
-            vx, vy, vz = get(VX, p), get(VY, p), get(VZ, p)
-            lam, mu, kept = lame[p, part], shear[p, part], keep[p, part]
-            exx, eyy, ezz = vx - get(VX, p - 1), vy - get(VY, p, -1), behind_z(vz)
-            spread = lam * (exx + eyy + ezz)
-            twice = 2.0 * mu
-            new = {
-                SXX: kept * get(SXX, p) + spread + twice * exx,
-                SYY: kept * get(SYY, p) + spread + twice * eyy,
-                SZZ: kept * get(SZZ, p) + spread + twice * ezz,
-                SXY: kept * get(SXY, p) + mu * (get(VX, p, 1) - vx + (get(VY, p + 1) - vy)),
-                SXZ: kept * get(SXZ, p) + mu * (ahead_z(vx) + (get(VZ, p + 1) - vz)),
-                SYZ: kept * get(SYZ, p) + mu * (ahead_z(vy) + (get(VZ, p, 1) - vz)),
-            }
-            if last:
-                new.update({VX: vx, VY: vy, VZ: vz})
-            if last:
-                return [(out, (f, p - x1), value) for f, value in new.items()]
-            return [(state, (f, p, rows), value) for f, value in new.items()]
-
-        each(low + 1, span - 2, stresses)
+    def speeds(p):
+        get = lambda f, q, shift=0: load(f, q, y0, y3, shift)
+        q = p + 1
+        sxy, sxz = get(SXY, p), get(SXZ, p)
+        vx = get(VX, p) + buoy[p] * (
+            get(SXX, q) - get(SXX, p) + (sxy - get(SXY, p, -1)) + behind_z(sxz))
+        syz = get(SYZ, q)
+        vy = get(VY, q) + buoy[q] * (
+            get(SXY, q) - sxy + (get(SYY, q, 1) - get(SYY, q)) + behind_z(syz))
+        vz = get(VZ, q) + buoy[q] * (
+            get(SXZ, q) - sxz + (syz - get(SYZ, q, -1)) + ahead_z(get(SZZ, q)))
+        return [(state, (VX, p, rows), vx), (state, (VY, q, rows), vy), (state, (VZ, q, rows), vz)]
+
+    def stresses(last, p):
+        a, b = (y1, y2) if last else (y0, y3)
+        get = lambda f, q, shift=0: load(f, q, a, b, shift)
+        part = slice(a - y0, b - y0)
+        vx, vy, vz = get(VX, p), get(VY, p), get(VZ, p)
+        lam, mu, kept = lame[p, part], shear[p, part], keep[p, part]
+        exx, eyy, ezz = vx - get(VX, p - 1), vy - get(VY, p, -1), behind_z(vz)
+        spread = lam * (exx + eyy + ezz)
+        twice = 2.0 * mu
+        new = {
+            SXX: kept * get(SXX, p) + spread + twice * exx,
+            SYY: kept * get(SYY, p) + spread + twice * eyy,
+            SZZ: kept * get(SZZ, p) + spread + twice * ezz,
+            SXY: kept * get(SXY, p) + mu * (get(VX, p, 1) - vx + (get(VY, p + 1) - vy)),
+            SXZ: kept * get(SXZ, p) + mu * (ahead_z(vx) + (get(VZ, p + 1) - vz)),
+            SYZ: kept * get(SYZ, p) + mu * (ahead_z(vy) + (get(VZ, p, 1) - vz)),
+        }
+        if last:
+            new.update({VX: vx, VY: vy, VZ: vz})
+        if last:
+            return [(out, (f, p - x1), value) for f, value in new.items()]
+        return [(state, (f, p, rows), value) for f, value in new.items()]
+
+    def together(body, places):
+        for ref, index, value in [store for p in places for store in body(p)]:
+            ref[index] = value
+
+    def sides(body, first, second):
+        @pl.loop(0, HALO // 2)
+        def _(turn):
+            together(body, [base + 2 * turn + extra for base in (first, second) for extra in (0, 1)])
+
+    def middle(body, first, after):
+        for p in range(first, after, 2):
+            together(body, range(p, min(p + 2, after)))
+
+    sent(0)
+    sent(1)
+    for done in range(STEPS):
+        middle(speeds, x1 + done, x2 - 1 - done)
+        if done == 0:
+            for index in range(2, len(parts)):
+                sent(index)
+        middle(functools.partial(stresses, False), x1 + 1 + done, x2 - 1 - done)
+
+    for index in range(1, len(parts)):
+        arrived(index)
+    for done in range(STEPS):
+        sides(speeds, x1 - HALO + done, x2 - 1 - done)
+        sides(functools.partial(stresses, done == STEPS - 1), x1 - HALO + 1 + done, x2 - 1 - done)
 
     for sends in direct:
         for key, copy in sends.items():

time: 21.4 us -> 18.8 us (0.88)
  Pallas kernels: 20.2 us -> 17.6 us
    pallas_call x1, Pallas kernels: 20.2 us -> 17.6 us  [on_device(): pl.pallas_call(functools.partial(kernel, nx, ny), out_shape=pltpu.VMEM(fi...]
where the time goes in v3:
time: 18.8 us; the launch traced here: 18.5 us
  Pallas kernels  17.6 us (94%)
  local copies, waits for them, and re-layouts  0.82 us (4%)
    pallas_call x1, Pallas kernels, on_device(): pl.pallas_call(functools.partial(kernel, nx, ny), out_shape=pltpu.VMEM(fi...  17.6 us
    unnamed x1, local copies, waits for them, and re-layouts  0.82 us

profile of v3, /device:TPU:9, one launch (start us, length us, event | category | flops | bytes accessed | tf_op | source)
XLA Modules:
  0.0 18.5 jit_solution(4116446274102010847)
XLA Ops:
  0.0 17.6 %waves.1 = f32[9,8,16,128]{3,2,1,0:T(8,128)S(1)} custom-call(f32[9,8,16,128]{3,2,1,0:T(8,128)} %fields.1, s32[8,16,128]{2,1,0:T(8,128)} %labels.1, f32[8]{0:T(128)} %buoy_t.1, f32[8]{0:T(128)} %lame_t.1, f32[8]{0:T(128)} %shear_t.1, f32[8]{0:T(128)} %relax_t.1), custom_call_target="tpu_custom_call" | custom-call | tf_op jit(solution)/shard_map/waves/pallas_call | solution.py:230
  17.6 0.8 %copy.8 = f32[9,8,16,128]{3,2,1,0:T(8,128)} copy(f32[9,8,16,128]{3,2,1,0:T(8,128)S(1)} %waves.1) | data formatting | bytes 1179648

commit v4 on v3

--- a/solution.py
+++ b/solution.py
@@ -106,7 +106,7 @@
     own[0].wait()
     arrived(0)
     rows = slice(y0, y3)
-    pack = 2 if local_x % 2 == 0 else 1
+    pack = 4 if local_x % 4 == 0 else 1
 
     def each(low, count, body):
         @pl.loop(0, count // pack)
@@ -191,9 +191,7 @@
             ref[index] = value
 
     def sides(body, first, second):
-        @pl.loop(0, HALO // 2)
-        def _(turn):
-            together(body, [base + 2 * turn + extra for base in (first, second) for extra in (0, 1)])
+        together(body, [base + extra for base in (first, second) for extra in range(HALO)])
 
     def middle(body, first, after):
         for p in range(first, after, 2):

time: 18.8 us -> 17.9 us (0.952)
  Pallas kernels: 17.6 us -> 16.7 us
    pallas_call x1, Pallas kernels: 17.6 us -> 16.7 us  [on_device(): pl.pallas_call(functools.partial(kernel, nx, ny), out_shape=pltpu.VMEM(fi...]
where the time goes in v4:
time: 17.9 us; the launch traced here: 17.5 us
  Pallas kernels  16.7 us (93%)
  local copies, waits for them, and re-layouts  0.82 us (5%)
    pallas_call x1, Pallas kernels, on_device(): pl.pallas_call(functools.partial(kernel, nx, ny), out_shape=pltpu.VMEM(fi...  16.7 us
    unnamed x1, local copies, waits for them, and re-layouts  0.82 us

profile of v4, /device:TPU:9, one launch (start us, length us, event | category | flops | bytes accessed | tf_op | source)
XLA Modules:
  0.0 17.5 jit_solution(934100576537406508)
XLA Ops:
  0.0 16.7 %waves.1 = f32[9,8,16,128]{3,2,1,0:T(8,128)S(1)} custom-call(f32[9,8,16,128]{3,2,1,0:T(8,128)} %fields.1, s32[8,16,128]{2,1,0:T(8,128)} %labels.1, f32[8]{0:T(128)} %buoy_t.1, f32[8]{0:T(128)} %lame_t.1, f32[8]{0:T(128)} %shear_t.1, f32[8]{0:T(128)} %relax_t.1), custom_call_target="tpu_custom_call" | custom-call | tf_op jit(solution)/shard_map/waves/pallas_call | solution.py:228
  16.7 0.8 %copy.8 = f32[9,8,16,128]{3,2,1,0:T(8,128)} copy(f32[9,8,16,128]{3,2,1,0:T(8,128)S(1)} %waves.1) | data formatting | bytes 1179648

commit v5 on v4

--- a/solution.py
+++ b/solution.py
@@ -12,7 +12,7 @@
 HALO = STEPS
 BASE = 8
 MESH = pl.DeviceIdType.MESH
-GROUPS = ((0, 3), (3, 6), (6, 9))
+GROUPS = ((0, 4), (4, 7), (7, 9))
 VX, VY, VZ, SXX, SYY, SZZ, SXY, SXZ, SYZ = range(9)
 
 
@@ -75,9 +75,12 @@
         direct.append({key: remote(*pair, *key) for key, pair in views(source, padded).items()})
         onward.append({key: remote(*pair, "gx", key[1]) for key, pair in corners(padded).items()})
 
-    for sends in direct:
-        for key, copy in sends.items():
-            pl.when(has[key])(copy.start)
+    for key, copy in direct[0].items():
+        pl.when(has[key])(copy.start)
+    for axis in ("gy", "gx"):
+        for sends in direct[1:]:
+            for way in (1, -1):
+                pl.when(has[axis, way])(sends[axis, way].start)
 
     def blank(a, b, c, d):
         state[:, a:b, c:d] = jnp.zeros((9, b - a, d - c, state.shape[3]), jnp.float32)

time: 17.9 us -> 17.9 us (level)
  no operation moved by 1% of the time
where the time goes in v5:
time: 17.9 us; the launch traced here: 17.5 us
  Pallas kernels  16.7 us (93%)
  local copies, waits for them, and re-layouts  0.82 us (5%)
    pallas_call x1, Pallas kernels, on_device(): pl.pallas_call(functools.partial(kernel, nx, ny), out_shape=pltpu.VMEM(fi...  16.7 us
    unnamed x1, local copies, waits for them, and re-layouts  0.82 us

profile of v5, /device:TPU:9, one launch (start us, length us, event | category | flops | bytes accessed | tf_op | source)
XLA Modules:
  0.0 17.5 jit_solution(8644017245004622509)
XLA Ops:
  0.0 16.7 %waves.1 = f32[9,8,16,128]{3,2,1,0:T(8,128)S(1)} custom-call(f32[9,8,16,128]{3,2,1,0:T(8,128)} %fields.1, s32[8,16,128]{2,1,0:T(8,128)} %labels.1, f32[8]{0:T(128)} %buoy_t.1, f32[8]{0:T(128)} %lame_t.1, f32[8]{0:T(128)} %shear_t.1, f32[8]{0:T(128)} %relax_t.1), custom_call_target="tpu_custom_call" | custom-call | tf_op jit(solution)/shard_map/waves/pallas_call | solution.py:231
  16.7 0.8 %copy.8 = f32[9,8,16,128]{3,2,1,0:T(8,128)} copy(f32[9,8,16,128]{3,2,1,0:T(8,128)S(1)} %waves.1) | data formatting | bytes 1179648
